TPU v7x, 128 devices: a whole 4x4x4 slice. The times are simulated.
128 devices in a mesh: gx: 8 (over x, core), gy: 16 (over z, y).
Axes of the slice: x: 4, y: 4, z: 4, core: 2. Of those that a mesh axis runs over, the one named last changes fastest.
Arguments:
- parent_fields: float32 [5, 4, 384, 6144], P(None, None, 'gx', 'gy'), may hold values from -6 to 6
- parent_velocity: float32 [2, 4, 384, 6144], P(None, None, 'gx', 'gy'), may hold values from -0.3 to 0.3
- parent_mixing: float32 [4, 384, 6144], P(None, 'gx', 'gy'), may hold values from 0.01 to 0.1
- nest_fields: float32 [5, 4, 384, 6144], P(None, None, 'gx', 'gy'), may hold values from -6 to 6
- nest_velocity: float32 [2, 4, 384, 6144], P(None, None, 'gx', 'gy'), may hold values from -0.3 to 0.3
- nest_mixing: float32 [4, 384, 6144], P(None, 'gx', 'gy'), may hold values from 0.01 to 0.1
- nest_anchor: int32 [2], replicated, may hold values from 1 to 3327, as said below
Outputs:
- parent_result: float32 [5, 4, 384, 6144], P(None, None, 'gx', 'gy')
- nest_result: float32 [5, 4, 384, 6144], P(None, None, 'gx', 'gy')
Inputs may be any that keep to these rules, and one draw needn't show every extreme that they name: `nest_anchor`: the row anchor is 1 to 254; the column anchor is 3073 to 3327, so the nest with a rim of one parent cell lies inside the parent grid.
All inputs are finite; a program needn't handle non-finite values.
Results may differ from a plain program's by a relative error of at most 0.00002.
Values sent between devices are 32-bit elements; how exact they have to be, the bound alone decides.
A program may use at most 192 MiB of HBM per device.

v0:
```python
import jax
import jax.numpy as jnp
from jax import lax
from jax.sharding import PartitionSpec as P

SUBSTEPS = 3
third = 1.0 / 3.0
two_thirds = 2.0 / 3.0
nudge_floor = 0.1
relax_width = 4.0


def shift_pairs(count, step):
    return [(i, i + step) for i in range(count) if 0 <= i + step < count]


def neighbours(cells):
    rows = lax.axis_size("gx")
    cols = lax.axis_size("gy")
    western = lax.ppermute(cells[:, :, -1:, :], "gx", shift_pairs(rows, 1))
    eastern = lax.ppermute(cells[:, :, :1, :], "gx", shift_pairs(rows, -1))
    southern = lax.ppermute(cells[:, :, :, -1:], "gy", shift_pairs(cols, 1))
    northern = lax.ppermute(cells[:, :, :, :1], "gy", shift_pairs(cols, -1))
    return (western, eastern, southern, northern)


def update(values, halo, velocity, mixing):
    west_row, east_row, south_col, north_col = halo
    western = jnp.concatenate([west_row, values[:, :, :-1, :]], axis=2)
    eastern = jnp.concatenate([values[:, :, 1:, :], east_row], axis=2)
    southern = jnp.concatenate([south_col, values[:, :, :, :-1]], axis=3)
    northern = jnp.concatenate([values[:, :, :, 1:], north_col], axis=3)
    along_rows = velocity[0]
    along_columns = velocity[1]
    upwind = (
        jnp.maximum(along_rows, 0.0) * (values - western)
        + jnp.minimum(along_rows, 0.0) * (eastern - values)
        + jnp.maximum(along_columns, 0.0) * (values - southern)
        + jnp.minimum(along_columns, 0.0) * (northern - values)
    )
    return values - upwind + mixing * (eastern + western + northern + southern - 4.0 * values)


def refine_rows(block):
    lower = block[:, :, :-2]
    centre = block[:, :, 1:-1]
    upper = block[:, :, 2:]
    stacked = jnp.stack(
        (third * lower + two_thirds * centre, centre, two_thirds * centre + third * upper), axis=3
    )
    extent = centre.shape
    return stacked.reshape(extent[0], extent[1], 3 * extent[2], extent[3])


def refine_columns(block):
    lower = block[:, :, :, :-2]
    centre = block[:, :, :, 1:-1]
    upper = block[:, :, :, 2:]
    stacked = jnp.stack(
        (third * lower + two_thirds * centre, centre, two_thirds * centre + third * upper), axis=4
    )
    extent = centre.shape
    return stacked.reshape(extent[0], extent[1], extent[2], 3 * extent[3])


def block_mean(state):
    extent = state.shape
    grouped = state.reshape(extent[0], extent[1], extent[2] // 3, 3, extent[3] // 3, 3)
    return jnp.sum(grouped, axis=(3, 5)) / 9.0


def relax_weight(row_global, column_global, total_rows, total_columns):
    row_distance = jnp.minimum(row_global, total_rows - 1 - row_global)
    column_distance = jnp.minimum(column_global, total_columns - 1 - column_global)
    distance = jnp.minimum(row_distance[:, None], column_distance[None, :]).astype(jnp.float32)
    return nudge_floor + (1.0 - nudge_floor) * jnp.exp(-distance / relax_width)


def within(positions, limit):
    return (positions >= 0) & (positions < limit)


def column_pairs(count, base, ratio, k, extra):
    pairs = []
    for m in range(count):
        j = ratio * m + k
        p = base + m + extra
        if j < count and p < count:
            pairs.append((p, j))
    return pairs


def per_device(
    parent_fields,
    parent_velocity,
    parent_mixing,
    nest_fields,
    nest_velocity,
    nest_mixing,
    nest_anchor,
):
    row_rank = lax.axis_index("gx")
    column_rank = lax.axis_index("gy")
    row_devices = lax.axis_size("gx")
    column_devices = lax.axis_size("gy")
    parent_rows = parent_fields.shape[2]
    parent_columns = parent_fields.shape[3]
    nest_rows = nest_fields.shape[2]
    nest_columns = nest_fields.shape[3]
    span_rows = nest_rows // 3
    span_columns = nest_columns // 3
    ratio = parent_columns // span_columns
    base = column_devices // 2
    base_column = base * parent_columns
    relay_rows = span_rows + 2
    relay_columns = span_columns + 2
    row_anchor = nest_anchor[0]
    column_anchor = nest_anchor[1]
    offset = column_anchor - 1 - base_column
    parent_next = update(parent_fields, neighbours(parent_fields), parent_velocity, parent_mixing)
    margin = parent_columns - span_columns
    wide = jnp.pad(parent_next, ((0, 0), (0, 0), (0, 0), (margin, margin)))
    relay_cols = None
    for k in range(ratio):
        for extra in (0, 1):
            if extra == 1 and k == 0:
                continue
            start = margin + span_columns * k + offset - extra * parent_columns
            piece = lax.dynamic_slice_in_dim(wide, start, relay_columns, axis=3)
            moved = lax.ppermute(piece, "gy", column_pairs(column_devices, base, ratio, k, extra))
            relay_cols = moved if relay_cols is None else relay_cols + moved
    padded = jnp.pad(relay_cols, ((0, 0), (0, 0), (relay_rows, relay_rows), (0, 0)))
    slots = []
    for target in range(row_devices):
        first = row_anchor - 1 + span_rows * target - parent_rows * row_rank
        first = jnp.clip(first, -relay_rows, parent_rows) + relay_rows
        slots.append(lax.dynamic_slice_in_dim(padded, first, relay_rows, axis=2))
    stacked = jnp.stack(slots, axis=0)
    relay = lax.psum_scatter(stacked, "gx", scatter_dimension=0, tiled=True)[0]
    forcing = refine_columns(refine_rows(relay))
    row_global = row_rank * nest_rows + jnp.arange(nest_rows, dtype=jnp.int32)
    column_global = column_rank * nest_columns + jnp.arange(nest_columns, dtype=jnp.int32)
    weight = relax_weight(
        row_global, column_global, row_devices * nest_rows, column_devices * nest_columns
    )
    state = nest_fields
    for substep in range(SUBSTEPS):
        moved = update(state, neighbours(state), nest_velocity, nest_mixing)
        state = moved + weight * (forcing - moved)
    coarse = block_mean(state)
    gathered = lax.all_gather(coarse, "gx", axis=2, tiled=True)
    total_span = row_devices * span_rows
    gathered = jnp.pad(gathered, ((0, 0), (0, 0), (parent_rows, parent_rows), (0, 0)))
    first = jnp.clip(parent_rows * row_rank - row_anchor, -parent_rows, total_span)
    strip = lax.dynamic_slice_in_dim(gathered, first + parent_rows, parent_rows, axis=2)
    pieces = []
    for extra in (1, 0):
        for k in range(ratio):
            if extra == 1 and k == 0:
                continue
            pairs = [(j, p) for p, j in column_pairs(column_devices, base, ratio, k, extra)]
            pieces.append(lax.ppermute(strip, "gy", pairs))
    joined = jnp.concatenate(pieces, axis=3)
    start = (ratio - 1) * span_columns - 1 - offset
    fed_back = lax.dynamic_slice_in_dim(joined, start, parent_columns, axis=3)
    relative_rows = row_rank * parent_rows + jnp.arange(parent_rows, dtype=jnp.int32) - row_anchor
    relative_columns = (
        column_rank * parent_columns + jnp.arange(parent_columns, dtype=jnp.int32) - column_anchor
    )
    rows_valid = within(relative_rows, total_span)
    columns_valid = within(relative_columns, column_devices * span_columns)
    covered = rows_valid[:, None] & columns_valid[None, :]
    parent_result = jnp.where(covered, fed_back, parent_next)
    return (parent_result, state)


def solution(mesh):
    placed = (
        P(None, None, "gx", "gy"),
        P(None, None, "gx", "gy"),
        P(None, "gx", "gy"),
        P(None, None, "gx", "gy"),
        P(None, None, "gx", "gy"),
        P(None, "gx", "gy"),
        P(),
    )
    return jax.shard_map(
        per_device,
        mesh=mesh,
        in_specs=placed,
        out_specs=(P(None, None, "gx", "gy"), P(None, None, "gx", "gy")),
        check_vma=False,
    )
```

profile of v0, /device:TPU:73, one launch (start us, length us, event | category | flops | bytes accessed | tf_op | source)
XLA Modules:
  0.0 439.8 jit_solution(16195591423806882408)
XLA Ops:
  7.2 2.4 fusion.26
  9.6 3.2 collective-permute-start.6
  12.8 2.1 collective-permute-start.7
  15.6 4.2 collective-permute-start.4
  20.4 1.9 collective-permute-start.5
  22.4 1.8 fusion.25
  24.1 2.1 fusion.27
  41.0 1.4 copy.336
  42.4 1.4 copy.337
  45.4 4.0 multiply_add_fusion.3
  49.4 1.4 pad_dynamic-slice_fusion.3
  50.8 2.1 collective-permute-start.10
  53.0 1.4 collective-permute-start.11
  54.3 1.4 collective-permute-start.12
  55.7 1.9 collective-permute-start.8
  59.9 1.9 fusion.21
  61.8 11.4 %collective-permute-done.10 = f32[5,4,48,130]{3,2,1,0:T(8,128)S(1)} collective-permute-done((f32[5,4,48,130]{3,2,1,0:T(8,128)S(1)}, f32[5,4,48,130]{3,2,1,0:T(8,128)S(1)}, u32[]{:S(2)}, u32[]{:S(2)}) %collective-permute-start.10) | collective-permute-done | bytes 499232 | tf_op jit(solution)/shard_map/ppermute | solution.py:130
  73.2 8.7 %collective-permute-start.2 = (f32[5,4,48,1]{3,2,1,0:T(8,128)}, f32[5,4,48,1]{3,2,1,0:T(8,128)}, u32[]{:S(2)}, u32[]{:S(2)}) collective-permute-start(f32[5,4,48,1]{3,2,1,0:T(8,128)} %get-tuple-element.30), channel_id=1, source_target_pairs={{0,1},{1,2},{2,3},{3,4},{4,5},{5,6},{6,7},{7,8},{8,9},{9,10},{10,1... | collective-permute-start | bytes 11528 | tf_op jit(solution)/shard_map/ppermute | solution.py:22
  81.9 20.6 %collective-permute-start.3 = (f32[5,4,48,1]{3,2,1,0:T(8,128)}, f32[5,4,48,1]{3,2,1,0:T(8,128)}, u32[]{:S(2)}, u32[]{:S(2)}) collective-permute-start(f32[5,4,48,1]{3,2,1,0:T(8,128)} %get-tuple-element.31), channel_id=1, source_target_pairs={{1,0},{2,1},{3,2},{4,3},{5,4},{6,5},{7,6},{8,7},{9,8},{10,9},{11,1... | collective-permute-start | bytes 11528 | tf_op jit(solution)/shard_map/ppermute | solution.py:23
  102.6 5.0 %collective-permute-start = (f32[5,4,1,384]{3,1,2,0:T(4,128)}, f32[5,4,1,384]{3,1,2,0:T(4,128)}, u32[]{:S(2)}, u32[]{:S(2)}) collective-permute-start(f32[5,4,1,384]{3,1,2,0:T(4,128)} %copy.336), channel_id=1, source_target_pairs={{0,16},{16,32},{32,48},{48,64},{64,80},{80,96},{96,112},{1,17},{17... | collective-permute-start | bytes 92168 | tf_op jit(solution)/shard_map/ppermute | solution.py:20
  107.6 1.9 collective-permute-start.1
  118.3 2.1 fusion.23
  121.8 1.4 copy.299
  123.1 1.4 copy.301
  124.5 81.9 %all-reduce.6.cloned.1.call-done = f32[8,5,4,18,130]{4,2,3,1,0:T(4,128)} async-done(((f32[8,5,4,18,130]{4,2,3,1,0:T(4,128)}), f32[8,5,4,18,130]{4,2,3,1,0:T(4,128)}) %all-reduce.6.cloned.1.call-update) | async-done | bytes 1497616
  206.4 1.7 dynamic-slice_bitcast_fusion
  209.7 3.6 copy.317
  213.3 3.4 copy.318
  216.8 4.1 multiply_add_fusion.2
  221.4 3.1 collective-permute-start.15
  224.5 2.2 collective-permute-start.16
  226.7 3.6 collective-permute-start.13
  230.4 2.8 collective-permute-start.14
  233.8 2.2 collective-permute-done.14
  236.4 1.8 multiply_add_fusion.1
  238.7 2.9 collective-permute-start.19
  241.5 3.1 collective-permute-start.20
  244.6 5.0 %collective-permute-start.17 = (f32[5,4,1,384]{3,1,2,0:T(4,128)S(1)}, f32[5,4,1,384]{3,1,2,0:T(4,128)S(1)}, u32[]{:S(2)}, u32[]{:S(2)}) collective-permute-start(f32[5,4,1,384]{3,1,2,0:T(4,128)S(1)} %copy.324), channel_id=1, source_target_pairs={{0,16},{16,32},{32,48},{48,64},{64,80},{80,96},{96,112},{1,17},{17... | collective-permute-start | bytes 92168 | tf_op jit(solution)/shard_map/ppermute | solution.py:20
  249.7 1.9 collective-permute-start.18
  252.2 3.0 collective-permute-done.18
  255.3 1.8 multiply_add_fusion
  257.1 60.9 %reshape.74 = f32[5,4,16,3,128,3]{5,4,3,2,1,0:T(8,128)} reshape(f32[5,4,48,384]{3,2,1,0:T(8,128)S(1)} %multiply_add_fusion) | data formatting | bytes 2949120 | tf_op jit(solution)/shard_map/reshape | solution.py:68
  318.0 20.5 %reduce_sum.9 = f32[5,4,16,128]{3,2,1,0:T(8,128)S(1)} reduce(f32[5,4,16,3,128,3]{5,4,3,2,1,0:T(8,128)} %reshape.74, f32[]{:T(128)} %constant.93.clone.1), dimensions={3,5}, to_apply=%region_1.2 | reduce | flops 327680 | bytes 1638404 | tf_op jit(solution)/shard_map/reduce_sum | solution.py:69
  339.9 32.5 %all-gather.2.cloned.1.call-done = f32[5,4,128,128]{3,1,0,2:T(4,128)} async-done(((f32[5,4,16,128]{3,1,0,2:T(4,128)}), f32[5,4,128,128]{3,1,0,2:T(4,128)}) %all-gather.2.cloned.1.call-update) | async-done | bytes 1310736 | tf_op jit(solution)/shard_map/all_gather | solution.py:151
  375.9 5.3 %collective-permute-start.23 = (f32[5,4,48,128]{3,2,1,0:T(8,128)S(1)}, f32[5,4,48,128]{3,2,1,0:T(8,128)S(1)}, u32[]{:S(2)}, u32[]{:S(2)}) collective-permute-start(f32[5,4,48,128]{3,2,1,0:T(8,128)S(1)} %copy.330), channel_id=1, source_target_pairs={{0,8},{3,9},{6,10},{9,11},{12,12},{15,13},{16,24},{19,25},{22,26},... | collective-permute-start | bytes 1474568 | tf_op jit(solution)/shard_map/ppermute | solution.py:162
  384.5 35.7 %collective-permute-done.21 = f32[5,4,48,128]{3,2,1,0:T(8,128)S(1)} collective-permute-done((f32[5,4,48,128]{3,2,1,0:T(8,128)S(1)}, f32[5,4,48,128]{3,2,1,0:T(8,128)S(1)}, u32[]{:S(2)}, u32[]{:S(2)}) %collective-permute-start.21) | collective-permute-done | bytes 491552 | tf_op jit(solution)/shard_map/ppermute | solution.py:162
  420.4 10.8 %collective-permute-done.25 = f32[5,4,48,128]{3,2,1,0:T(8,128)S(1)} collective-permute-done((f32[5,4,48,128]{3,2,1,0:T(8,128)S(1)}, f32[5,4,48,128]{3,2,1,0:T(8,128)S(1)}, u32[]{:S(2)}, u32[]{:S(2)}) %collective-permute-start.25) | collective-permute-done | bytes 491552 | tf_op jit(solution)/shard_map/ppermute | solution.py:162
  431.3 1.6 dynamic-slice_select_fusion
  (113 shorter events, 30.2 us)
Async XLA Ops:
  7.2 7.7 %copy-start = (f32[5,4,48,384]{3,2,1,0:T(8,128)S(1)}, f32[5,4,48,384]{3,2,1,0:T(8,128)}, u32[]{:S(2)}) copy-start(f32[5,4,48,384]{3,2,1,0:T(8,128)} %param.7) | copy-start | bytes 4423684
  7.2 199.3 %all-reduce.6.cloned.1.call-start = ((), (), s32[]{:S(2)}) async-start(), calls=%async_computation.1 | async-start | bytes 5898240
  9.6 35.7 %collective-permute-start.6 = (f32[5,4,48,1]{3,2,1,0:T(8,128)}, f32[5,4,48,1]{3,2,1,0:T(8,128)}, u32[]{:S(2)}, u32[]{:S(2)}) collective-permute-start(f32[5,4,48,1]{3,2,1,0:T(8,128)} %get-tuple-element.43), channel_id=1, source_target_pairs={{0,1},{1,2},{2,3},{3,4},{4,5},{5,6},{6,7},{7,8},{8,9},{9,10},{10,1... | collective-permute-start | bytes 11528 | tf_op jit(solution)/shard_map/ppermute | solution.py:22
  12.8 32.5 %collective-permute-start.7 = (f32[5,4,48,1]{3,2,1,0:T(8,128)}, f32[5,4,48,1]{3,2,1,0:T(8,128)}, u32[]{:S(2)}, u32[]{:S(2)}) collective-permute-start(f32[5,4,48,1]{3,2,1,0:T(8,128)} %get-tuple-element.44), channel_id=1, source_target_pairs={{1,0},{2,1},{3,2},{4,3},{5,4},{6,5},{7,6},{8,7},{9,8},{10,9},{11,1... | collective-permute-start | bytes 11528 | tf_op jit(solution)/shard_map/ppermute | solution.py:23
  15.6 28.2 %collective-permute-start.4 = (f32[5,4,1,384]{3,1,2,0:T(4,128)}, f32[5,4,1,384]{3,1,2,0:T(4,128)}, u32[]{:S(2)}, u32[]{:S(2)}) collective-permute-start(f32[5,4,1,384]{3,1,2,0:T(4,128)} %copy.338), channel_id=1, source_target_pairs={{0,16},{16,32},{32,48},{48,64},{64,80},{80,96},{96,112},{1,17},{17... | collective-permute-start | bytes 92168 | tf_op jit(solution)/shard_map/ppermute | solution.py:20
  20.4 24.1 %collective-permute-start.5 = (f32[5,4,1,384]{3,1,2,0:T(4,128)}, f32[5,4,1,384]{3,1,2,0:T(4,128)}, u32[]{:S(2)}, u32[]{:S(2)}) collective-permute-start(f32[5,4,1,384]{3,1,2,0:T(4,128)} %copy.339), channel_id=1, source_target_pairs={{16,0},{32,16},{48,32},{64,48},{80,64},{96,80},{112,96},{17,1},{33... | collective-permute-start | bytes 92168 | tf_op jit(solution)/shard_map/ppermute | solution.py:21
  24.1 2.1 copy-start.1
  26.2 1.8 copy-start.9
  26.2 2.7 copy-start.11
  49.4 1.4 copy-start.2
  49.4 9.6 %copy-start.10 = (f32[2,4,48,384]{3,2,1,0:T(8,128)S(1)}, f32[2,4,48,384]{3,2,1,0:T(8,128)}, u32[]{:S(2)}) copy-start(f32[2,4,48,384]{3,2,1,0:T(8,128)} %param.11) | copy-start | bytes 1769476
  50.8 22.4 %collective-permute-start.10 = (f32[5,4,48,130]{3,2,1,0:T(8,128)S(1)}, f32[5,4,48,130]{3,2,1,0:T(8,128)S(1)}, u32[]{:S(2)}, u32[]{:S(2)}) collective-permute-start(f32[5,4,48,130]{3,2,1,0:T(8,128)S(1)} %get-tuple-element.35), channel_id=1, source_target_pairs={{9,1},{10,4},{11,7},{12,10},{13,13},{25,17},{26,20},{27,23},{28,26... | collective-permute-start | bytes 1497608 | tf_op jit(solution)/shard_map/ppermute | solution.py:130
  53.0 29.0 %collective-permute-start.11 = (f32[5,4,48,130]{3,2,1,0:T(8,128)S(1)}, f32[5,4,48,130]{3,2,1,0:T(8,128)S(1)}, u32[]{:S(2)}, u32[]{:S(2)}) collective-permute-start(f32[5,4,48,130]{3,2,1,0:T(8,128)S(1)} %get-tuple-element.36), channel_id=1, source_target_pairs={{8,2},{9,5},{10,8},{11,11},{12,14},{24,18},{25,21},{26,24},{27,27}... | collective-permute-start | bytes 1497608 | tf_op jit(solution)/shard_map/ppermute | solution.py:130
  54.3 48.2 %collective-permute-start.12 = (f32[5,4,48,130]{3,2,1,0:T(8,128)S(1)}, f32[5,4,48,130]{3,2,1,0:T(8,128)S(1)}, u32[]{:S(2)}, u32[]{:S(2)}) collective-permute-start(f32[5,4,48,130]{3,2,1,0:T(8,128)S(1)} %get-tuple-element.37), channel_id=1, source_target_pairs={{9,2},{10,5},{11,8},{12,11},{13,14},{25,18},{26,21},{27,24},{28,27... | collective-permute-start | bytes 1497608 | tf_op jit(solution)/shard_map/ppermute | solution.py:130
  55.7 51.9 %collective-permute-start.8 = (f32[5,4,48,130]{3,2,1,0:T(8,128)S(1)}, f32[5,4,48,130]{3,2,1,0:T(8,128)S(1)}, u32[]{:S(2)}, u32[]{:S(2)}) collective-permute-start(f32[5,4,48,130]{3,2,1,0:T(8,128)S(1)} %get-tuple-element.38), channel_id=1, source_target_pairs={{8,0},{9,3},{10,6},{11,9},{12,12},{13,15},{24,16},{25,19},{26,22},... | collective-permute-start | bytes 1497608 | tf_op jit(solution)/shard_map/ppermute | solution.py:130
  57.6 52.0 %collective-permute-start.9 = (f32[5,4,48,130]{3,2,1,0:T(8,128)S(1)}, f32[5,4,48,130]{3,2,1,0:T(8,128)S(1)}, u32[]{:S(2)}, u32[]{:S(2)}) collective-permute-start(f32[5,4,48,130]{3,2,1,0:T(8,128)S(1)} %get-tuple-element.34), channel_id=1, source_target_pairs={{8,1},{9,4},{10,7},{11,10},{12,13},{24,17},{25,20},{26,23},{27,26}... | collective-permute-start | bytes 1497608 | tf_op jit(solution)/shard_map/ppermute | solution.py:130
  73.2 143.6 %collective-permute-start.2 = (f32[5,4,48,1]{3,2,1,0:T(8,128)}, f32[5,4,48,1]{3,2,1,0:T(8,128)}, u32[]{:S(2)}, u32[]{:S(2)}) collective-permute-start(f32[5,4,48,1]{3,2,1,0:T(8,128)} %get-tuple-element.30), channel_id=1, source_target_pairs={{0,1},{1,2},{2,3},{3,4},{4,5},{5,6},{6,7},{7,8},{8,9},{9,10},{10,1... | collective-permute-start | bytes 11528 | tf_op jit(solution)/shard_map/ppermute | solution.py:22
  81.9 134.8 %collective-permute-start.3 = (f32[5,4,48,1]{3,2,1,0:T(8,128)}, f32[5,4,48,1]{3,2,1,0:T(8,128)}, u32[]{:S(2)}, u32[]{:S(2)}) collective-permute-start(f32[5,4,48,1]{3,2,1,0:T(8,128)} %get-tuple-element.31), channel_id=1, source_target_pairs={{1,0},{2,1},{3,2},{4,3},{5,4},{6,5},{7,6},{8,7},{9,8},{10,9},{11,1... | collective-permute-start | bytes 11528 | tf_op jit(solution)/shard_map/ppermute | solution.py:23
  102.6 19.2 %collective-permute-start = (f32[5,4,1,384]{3,1,2,0:T(4,128)}, f32[5,4,1,384]{3,1,2,0:T(4,128)}, u32[]{:S(2)}, u32[]{:S(2)}) collective-permute-start(f32[5,4,1,384]{3,1,2,0:T(4,128)} %copy.336), channel_id=1, source_target_pairs={{0,16},{16,32},{32,48},{48,64},{64,80},{80,96},{96,112},{1,17},{17... | collective-permute-start | bytes 92168 | tf_op jit(solution)/shard_map/ppermute | solution.py:20
  107.6 15.5 %collective-permute-start.1 = (f32[5,4,1,384]{3,1,2,0:T(4,128)}, f32[5,4,1,384]{3,1,2,0:T(4,128)}, u32[]{:S(2)}, u32[]{:S(2)}) collective-permute-start(f32[5,4,1,384]{3,1,2,0:T(4,128)} %copy.337), channel_id=1, source_target_pairs={{16,0},{32,16},{48,32},{64,48},{80,64},{96,80},{112,96},{17,1},{33... | collective-permute-start | bytes 92168 | tf_op jit(solution)/shard_map/ppermute | solution.py:21
  118.0 254.4 %all-gather.2.cloned.1.call-start = ((), (), s32[]{:S(2)}) async-start(), calls=%async_computation | async-start | bytes 1474560 | tf_op jit(solution)/shard_map/all_gather | solution.py:151
  118.3 2.8 copy-start.12
  221.4 14.6 %collective-permute-start.15 = (f32[5,4,48,1]{3,2,1,0:T(8,128)S(1)}, f32[5,4,48,1]{3,2,1,0:T(8,128)S(1)}, u32[]{:S(2)}, u32[]{:S(2)}) collective-permute-start(f32[5,4,48,1]{3,2,1,0:T(8,128)S(1)} %get-tuple-element.22), channel_id=1, source_target_pairs={{0,1},{1,2},{2,3},{3,4},{4,5},{5,6},{6,7},{7,8},{8,9},{9,10},{10,1... | collective-permute-start | bytes 11528 | tf_op jit(solution)/shard_map/ppermute | solution.py:22
  224.5 11.8 %collective-permute-start.16 = (f32[5,4,48,1]{3,2,1,0:T(8,128)S(1)}, f32[5,4,48,1]{3,2,1,0:T(8,128)S(1)}, u32[]{:S(2)}, u32[]{:S(2)}) collective-permute-start(f32[5,4,48,1]{3,2,1,0:T(8,128)S(1)} %get-tuple-element.23), channel_id=1, source_target_pairs={{1,0},{2,1},{3,2},{4,3},{5,4},{6,5},{7,6},{8,7},{9,8},{10,9},{11,1... | collective-permute-start | bytes 11528 | tf_op jit(solution)/shard_map/ppermute | solution.py:23
  226.7 7.0 %collective-permute-start.13 = (f32[5,4,1,384]{3,1,2,0:T(4,128)S(1)}, f32[5,4,1,384]{3,1,2,0:T(4,128)S(1)}, u32[]{:S(2)}, u32[]{:S(2)}) collective-permute-start(f32[5,4,1,384]{3,1,2,0:T(4,128)S(1)} %copy.319), channel_id=1, source_target_pairs={{0,16},{16,32},{32,48},{48,64},{64,80},{80,96},{96,112},{1,17},{17... | collective-permute-start | bytes 92168 | tf_op jit(solution)/shard_map/ppermute | solution.py:20
  230.3 6.0 %copy-start.5 = (f32[4,48,384]{2,1,0:T(8,128)S(1)}, f32[4,48,384]{2,1,0:T(8,128)}, u32[]{:S(2)}) copy-start(f32[4,48,384]{2,1,0:T(8,128)} %get-tuple-element.60) | copy-start | bytes 884740
  230.4 6.0 %copy-start.6 = (f32[4,48,384]{2,1,0:T(8,128)S(1)}, f32[4,48,384]{2,1,0:T(8,128)}, u32[]{:S(2)}) copy-start(f32[4,48,384]{2,1,0:T(8,128)} %get-tuple-element.61) | copy-start | bytes 884740
  230.4 6.0 %copy-start.7 = (f32[4,48,384]{2,1,0:T(8,128)S(1)}, f32[4,48,384]{2,1,0:T(8,128)}, u32[]{:S(2)}) copy-start(f32[4,48,384]{2,1,0:T(8,128)} %param.12) | copy-start | bytes 884740
  230.4 6.0 %copy-start.8 = (f32[48,384]{1,0:T(8,128)S(1)}, f32[48,384]{1,0:T(8,128)}, u32[]{:S(2)}) copy-start(f32[48,384]{1,0:T(8,128)} %multiply_add_fusion.4) | copy-start | bytes 221188
  230.4 5.6 %collective-permute-start.14 = (f32[5,4,1,384]{3,1,2,0:T(4,128)S(1)}, f32[5,4,1,384]{3,1,2,0:T(4,128)S(1)}, u32[]{:S(2)}, u32[]{:S(2)}) collective-permute-start(f32[5,4,1,384]{3,1,2,0:T(4,128)S(1)} %copy.321), channel_id=1, source_target_pairs={{16,0},{32,16},{48,32},{64,48},{80,64},{96,80},{112,96},{17,1},{33... | collective-permute-start | bytes 92168 | tf_op jit(solution)/shard_map/ppermute | solution.py:21
  238.7 16.6 %collective-permute-start.19 = (f32[5,4,48,1]{3,2,1,0:T(8,128)S(1)}, f32[5,4,48,1]{3,2,1,0:T(8,128)S(1)}, u32[]{:S(2)}, u32[]{:S(2)}) collective-permute-start(f32[5,4,48,1]{3,2,1,0:T(8,128)S(1)} %get-tuple-element.14), channel_id=1, source_target_pairs={{0,1},{1,2},{2,3},{3,4},{4,5},{5,6},{6,7},{7,8},{8,9},{9,10},{10,1... | collective-permute-start | bytes 11528 | tf_op jit(solution)/shard_map/ppermute | solution.py:22
  241.5 13.7 %collective-permute-start.20 = (f32[5,4,48,1]{3,2,1,0:T(8,128)S(1)}, f32[5,4,48,1]{3,2,1,0:T(8,128)S(1)}, u32[]{:S(2)}, u32[]{:S(2)}) collective-permute-start(f32[5,4,48,1]{3,2,1,0:T(8,128)S(1)} %get-tuple-element.15), channel_id=1, source_target_pairs={{1,0},{2,1},{3,2},{4,3},{5,4},{6,5},{7,6},{8,7},{9,8},{10,9},{11,1... | collective-permute-start | bytes 11528 | tf_op jit(solution)/shard_map/ppermute | solution.py:23
  244.6 7.5 %collective-permute-start.17 = (f32[5,4,1,384]{3,1,2,0:T(4,128)S(1)}, f32[5,4,1,384]{3,1,2,0:T(4,128)S(1)}, u32[]{:S(2)}, u32[]{:S(2)}) collective-permute-start(f32[5,4,1,384]{3,1,2,0:T(4,128)S(1)} %copy.324), channel_id=1, source_target_pairs={{0,16},{16,32},{32,48},{48,64},{64,80},{80,96},{96,112},{1,17},{17... | collective-permute-start | bytes 92168 | tf_op jit(solution)/shard_map/ppermute | solution.py:20
  249.7 5.5 %collective-permute-start.18 = (f32[5,4,1,384]{3,1,2,0:T(4,128)S(1)}, f32[5,4,1,384]{3,1,2,0:T(4,128)S(1)}, u32[]{:S(2)}, u32[]{:S(2)}) collective-permute-start(f32[5,4,1,384]{3,1,2,0:T(4,128)S(1)} %copy.326), channel_id=1, source_target_pairs={{16,0},{32,16},{48,32},{64,48},{80,64},{96,80},{112,96},{17,1},{33... | collective-permute-start | bytes 92168 | tf_op jit(solution)/shard_map/ppermute | solution.py:21
  257.1 61.0 %copy-start.4 = (f32[5,4,48,384]{3,2,1,0:T(8,128)}, f32[5,4,48,384]{3,2,1,0:T(8,128)S(1)}, u32[]{:S(2)}) copy-start(f32[5,4,48,384]{3,2,1,0:T(8,128)S(1)} %multiply_add_fusion) | copy-start | bytes 4423684
  372.6 47.6 %collective-permute-start.21 = (f32[5,4,48,128]{3,2,1,0:T(8,128)S(1)}, f32[5,4,48,128]{3,2,1,0:T(8,128)S(1)}, u32[]{:S(2)}, u32[]{:S(2)}) collective-permute-start(f32[5,4,48,128]{3,2,1,0:T(8,128)S(1)} %copy.330), channel_id=1, source_target_pairs={{1,9},{4,10},{7,11},{10,12},{13,13},{17,25},{20,26},{23,27},{26,28... | collective-permute-start | bytes 1474568 | tf_op jit(solution)/shard_map/ppermute | solution.py:162
  373.9 46.4 %collective-permute-start.22 = (f32[5,4,48,128]{3,2,1,0:T(8,128)S(1)}, f32[5,4,48,128]{3,2,1,0:T(8,128)S(1)}, u32[]{:S(2)}, u32[]{:S(2)}) collective-permute-start(f32[5,4,48,128]{3,2,1,0:T(8,128)S(1)} %copy.330), channel_id=1, source_target_pairs={{2,9},{5,10},{8,11},{11,12},{14,13},{18,25},{21,26},{24,27},{27,28... | collective-permute-start | bytes 1474568 | tf_op jit(solution)/shard_map/ppermute | solution.py:162
  375.9 44.5 %collective-permute-start.23 = (f32[5,4,48,128]{3,2,1,0:T(8,128)S(1)}, f32[5,4,48,128]{3,2,1,0:T(8,128)S(1)}, u32[]{:S(2)}, u32[]{:S(2)}) collective-permute-start(f32[5,4,48,128]{3,2,1,0:T(8,128)S(1)} %copy.330), channel_id=1, source_target_pairs={{0,8},{3,9},{6,10},{9,11},{12,12},{15,13},{16,24},{19,25},{22,26},... | collective-permute-start | bytes 1474568 | tf_op jit(solution)/shard_map/ppermute | solution.py:162
  381.8 38.6 %collective-permute-start.24 = (f32[5,4,48,128]{3,2,1,0:T(8,128)S(1)}, f32[5,4,48,128]{3,2,1,0:T(8,128)S(1)}, u32[]{:S(2)}, u32[]{:S(2)}) collective-permute-start(f32[5,4,48,128]{3,2,1,0:T(8,128)S(1)} %copy.330), channel_id=1, source_target_pairs={{1,8},{4,9},{7,10},{10,11},{13,12},{17,24},{20,25},{23,26},{26,27}... | collective-permute-start | bytes 1474568 | tf_op jit(solution)/shard_map/ppermute | solution.py:162
  383.2 48.1 %collective-permute-start.25 = (f32[5,4,48,128]{3,2,1,0:T(8,128)S(1)}, f32[5,4,48,128]{3,2,1,0:T(8,128)S(1)}, u32[]{:S(2)}, u32[]{:S(2)}) collective-permute-start(f32[5,4,48,128]{3,2,1,0:T(8,128)S(1)} %copy.330), channel_id=1, source_target_pairs={{2,8},{5,9},{8,10},{11,11},{14,12},{18,24},{21,25},{24,26},{27,27}... | collective-permute-start | bytes 1474568 | tf_op jit(solution)/shard_map/ppermute | solution.py:162
  420.3 11.0 %copy-start.3 = (f32[5,4,48,384]{3,2,1,0:T(8,128)S(1)}, f32[5,4,48,384]{3,2,1,0:T(8,128)}, u32[]{:S(2)}) copy-start(f32[5,4,48,384]{3,2,1,0:T(8,128)} %copy-done.2) | copy-start | bytes 4423684
Sparse Core Ops, SparseCore 0:
  118.2 88.2 all-reduce.5
  339.4 32.9 all-gather.1
where the time goes:
time: 441 us; the launch traced here: 440 us
  waiting for transfers between devices  178 us (40%)
  local copies, waits for them, and re-layouts  104 us (24%)
  starting transfers between devices  91.2 us (21%)
  other arithmetic  39.5 us (9%)
  between operations  27 us (6%)
    unnamed x3, waiting for transfers between devices  81.9 us
    reshape x1, local copies, waits for them, and re-layouts, block_mean(): state.reshape(extent[0], extent[1], extent[2] // 3, 3, extent[3] // 3, 3)  60.9 us
    ppermute x5, waiting for transfers between devices, per_device(): pieces.append(lax.ppermute(strip, 'gy', pairs))  46.6 us
    all_gather x1, waiting for transfers between devices, per_device(): gathered = lax.all_gather(coarse, 'gx', axis=2, tiled=True)  32.5 us
    ppermute x4, starting transfers between devices, neighbours(): northern = lax.ppermute(cells[:, :, :, :1], 'gy', shift_pairs(cols, -1))  28 us
    reduce_sum x1, other arithmetic, block_mean(): return jnp.sum(grouped, axis=(3, 5)) / 9.0  20.5 us
    ppermute x4, starting transfers between devices, neighbours(): southern = lax.ppermute(cells[:, :, :, -1:], 'gy', shift_pairs(cols, 1))  17.9 us
    ppermute x4, starting transfers between devices, neighbours(): western = lax.ppermute(cells[:, :, -1:, :], 'gx', shift_pairs(rows, 1))  17.9 us
  transfers between devices with their start and end apart: 28, of which 8 were waited for; matrix products, arithmetic and copies ran while one was open for 10% of the time, Pallas kernels for 0%

commit v1 on v0

--- a/solution.py
+++ b/solution.py
@@ -148,7 +148,9 @@
         moved = update(state, neighbours(state), nest_velocity, nest_mixing)
         state = moved + weight * (forcing - moved)
     coarse = block_mean(state)
-    gathered = lax.all_gather(coarse, "gx", axis=2, tiled=True)
+    gathered = jnp.concatenate(
+        lax.all_to_all(jnp.stack([coarse] * lax.axis_size("gx")), "gx", 0, 0), axis=2
+    )
     total_span = row_devices * span_rows
     gathered = jnp.pad(gathered, ((0, 0), (0, 0), (parent_rows, parent_rows), (0, 0)))
     first = jnp.clip(parent_rows * row_rank - row_anchor, -parent_rows, total_span)

time: 441 us -> 439 us (level)
  waiting for transfers between devices: 178 us -> 164 us
  starting transfers between devices: 91.2 us -> 103 us
    all_gather x1 -> x0, waiting for transfers between devices: 32.5 us -> none  [per_device(): gathered = lax.all_gather(coarse, 'gx', axis=2, tiled=True)]
    all_to_all x0 -> x1, waiting for transfers between devices: none -> 17.3 us  [per_device(): lax.all_to_all(jnp.stack([coarse] * lax.axis_size('gx')), 'gx', 0, 0)]
    all_to_all x0 -> x1, starting transfers between devices: none -> 11 us  [per_device(): lax.all_to_all(jnp.stack([coarse] * lax.axis_size('gx')), 'gx', 0, 0)]
    unnamed x3 -> x2, waiting for transfers between devices: 81.9 us -> 83.5 us
    unnamed x42 -> x44, local copies, waits for them, and re-layouts: 11 us -> 11 us
  transfers between devices with their start and end apart: 28 -> 28, of which waited for: 8 -> 8; matrix products, arithmetic and copies ran while one was open for 10% -> 9% of each run, Pallas kernels for 0% -> 0%
where the time goes in v1:
time: 439 us; the launch traced here: 438 us
  waiting for transfers between devices  164 us (37%)
  local copies, waits for them, and re-layouts  104 us (24%)
  starting transfers between devices  103 us (23%)
  other arithmetic  40.4 us (9%)
  between operations  27 us (6%)
    unnamed x2, waiting for transfers between devices  83.5 us
    reshape x1, local copies, waits for them, and re-layouts, block_mean(): state.reshape(extent[0], extent[1], extent[2] // 3, 3, extent[3] // 3, 3)  61.7 us
    ppermute x5, waiting for transfers between devices, per_device(): pieces.append(lax.ppermute(strip, 'gy', pairs))  46 us
    ppermute x4, starting transfers between devices, neighbours(): northern = lax.ppermute(cells[:, :, :, :1], 'gy', shift_pairs(cols, -1))  28 us
    reduce_sum x1, other arithmetic, block_mean(): return jnp.sum(grouped, axis=(3, 5)) / 9.0  20.5 us
    ppermute x4, starting transfers between devices, neighbours(): southern = lax.ppermute(cells[:, :, :, -1:], 'gy', shift_pairs(cols, 1))  17.9 us
    ppermute x4, starting transfers between devices, neighbours(): western = lax.ppermute(cells[:, :, -1:, :], 'gx', shift_pairs(rows, 1))  17.9 us
    all_to_all x1, waiting for transfers between devices, per_device(): lax.all_to_all(jnp.stack([coarse] * lax.axis_size('gx')), 'gx', 0, 0)  17.3 us
  transfers between devices with their start and end apart: 28, of which 8 were waited for; matrix products, arithmetic and copies ran while one was open for 9% of the time, Pallas kernels for 0%

profile of v1, /device:TPU:73, one launch (start us, length us, event | category | flops | bytes accessed | tf_op | source)
XLA Modules:
  0.0 437.6 jit_solution(17489004870840350718)
XLA Ops:
  7.2 2.4 fusion.26
  9.6 3.2 collective-permute-start.6
  12.8 2.1 collective-permute-start.7
  15.6 4.2 collective-permute-start.4
  20.4 1.9 collective-permute-start.5
  22.4 1.8 fusion.25
  24.1 2.1 fusion.27
  41.0 1.4 copy.322
  42.4 1.4 copy.323
  45.4 4.0 multiply_add_fusion.3
  49.4 1.4 pad_dynamic-slice_fusion.3
  50.8 2.1 collective-permute-start.10
  53.0 1.4 collective-permute-start.11
  54.3 1.4 collective-permute-start.12
  55.7 1.9 collective-permute-start.8
  57.6 1.4 collective-permute-start.9
  59.9 1.9 fusion.21
  61.8 11.4 %collective-permute-done.10 = f32[5,4,48,130]{3,2,1,0:T(8,128)S(1)} collective-permute-done((f32[5,4,48,130]{3,2,1,0:T(8,128)S(1)}, f32[5,4,48,130]{3,2,1,0:T(8,128)S(1)}, u32[]{:S(2)}, u32[]{:S(2)}) %collective-permute-start.10) | collective-permute-done | bytes 499232 | tf_op jit(solution)/shard_map/ppermute | solution.py:130
  73.2 8.7 %collective-permute-start.2 = (f32[5,4,48,1]{3,2,1,0:T(8,128)}, f32[5,4,48,1]{3,2,1,0:T(8,128)}, u32[]{:S(2)}, u32[]{:S(2)}) collective-permute-start(f32[5,4,48,1]{3,2,1,0:T(8,128)} %get-tuple-element.30), channel_id=1, source_target_pairs={{0,1},{1,2},{2,3},{3,4},{4,5},{5,6},{6,7},{7,8},{8,9},{9,10},{10,1... | collective-permute-start | bytes 11528 | tf_op jit(solution)/shard_map/ppermute | solution.py:22
  81.9 20.6 %collective-permute-start.3 = (f32[5,4,48,1]{3,2,1,0:T(8,128)}, f32[5,4,48,1]{3,2,1,0:T(8,128)}, u32[]{:S(2)}, u32[]{:S(2)}) collective-permute-start(f32[5,4,48,1]{3,2,1,0:T(8,128)} %get-tuple-element.31), channel_id=1, source_target_pairs={{1,0},{2,1},{3,2},{4,3},{5,4},{6,5},{7,6},{8,7},{9,8},{10,9},{11,1... | collective-permute-start | bytes 11528 | tf_op jit(solution)/shard_map/ppermute | solution.py:23
  102.6 5.0 %collective-permute-start = (f32[5,4,1,384]{3,1,2,0:T(4,128)S(1)}, f32[5,4,1,384]{3,1,2,0:T(4,128)S(1)}, u32[]{:S(2)}, u32[]{:S(2)}) collective-permute-start(f32[5,4,1,384]{3,1,2,0:T(4,128)S(1)} %copy-done.11), channel_id=1, source_target_pairs={{0,16},{16,32},{32,48},{48,64},{64,80},{80,96},{96,112},{1,17},{17... | collective-permute-start | bytes 92168 | tf_op jit(solution)/shard_map/ppermute | solution.py:20
  107.7 2.1 collective-permute-start.1
  118.3 2.1 fusion.23
  123.0 83.5 %all-reduce.6.cloned.1.call-done = f32[8,5,4,18,130]{4,2,3,1,0:T(4,128)} async-done(((f32[8,5,4,18,130]{4,2,3,1,0:T(4,128)}), f32[8,5,4,18,130]{4,2,3,1,0:T(4,128)}) %all-reduce.6.cloned.1.call-update) | async-done | bytes 1497616
  206.5 1.6 dynamic-slice_bitcast_fusion
  209.7 3.6 copy.308
  213.3 3.4 copy.309
  216.7 4.1 multiply_add_fusion.2
  221.3 3.1 collective-permute-start.15
  224.5 2.2 collective-permute-start.16
  226.7 3.6 collective-permute-start.13
  230.3 2.8 collective-permute-start.14
  233.7 2.2 collective-permute-done.14
  236.3 1.8 multiply_add_fusion.1
  238.6 2.9 collective-permute-start.19
  241.5 3.1 collective-permute-start.20
  244.6 5.0 %collective-permute-start.17 = (f32[5,4,1,384]{3,1,2,0:T(4,128)S(1)}, f32[5,4,1,384]{3,1,2,0:T(4,128)S(1)}, u32[]{:S(2)}, u32[]{:S(2)}) collective-permute-start(f32[5,4,1,384]{3,1,2,0:T(4,128)S(1)} %copy.315), channel_id=1, source_target_pairs={{0,16},{16,32},{32,48},{48,64},{64,80},{80,96},{96,112},{1,17},{17... | collective-permute-start | bytes 92168 | tf_op jit(solution)/shard_map/ppermute | solution.py:20
  249.6 2.1 collective-permute-start.18
  252.3 2.8 collective-permute-done.18
  255.2 2.6 multiply_add_fusion
  257.8 61.7 %reshape.82 = f32[5,4,16,3,128,3]{5,4,3,2,1,0:T(8,128)} reshape(f32[5,4,48,384]{3,2,1,0:T(8,128)} %multiply_add_fusion) | data formatting | bytes 2949120 | tf_op jit(solution)/shard_map/reshape | solution.py:68
  319.5 20.5 %reduce_sum.9 = f32[5,4,16,128]{3,2,1,0:T(8,128)S(1)} reduce(f32[5,4,16,3,128,3]{5,4,3,2,1,0:T(8,128)} %reshape.82, f32[]{:T(128)} %constant.93.clone.1), dimensions={3,5}, to_apply=%region_1.2 | reduce | flops 327680 | bytes 1638404 | tf_op jit(solution)/shard_map/reduce_sum | solution.py:69
  341.3 11.0 %all-to-all-start = ((f32[8,5,4,16,128]{4,3,2,1,0:T(8,128)}), f32[8,5,4,16,128]{4,3,2,1,0:T(8,128)S(1)}, u32[]{:S(2)}, u32[]{:S(2)}) async-start(f32[8,5,4,16,128]{4,3,2,1,0:T(8,128)} %stack.79), calls=%async_computation | async-start | bytes 2621440 | tf_op jit(solution)/shard_map/all_to_all | solution.py:152
  352.9 17.3 %all-to-all-done = f32[8,5,4,16,128]{4,3,2,1,0:T(8,128)S(1)} async-done(((f32[8,5,4,16,128]{4,3,2,1,0:T(8,128)}), f32[8,5,4,16,128]{4,3,2,1,0:T(8,128)S(1)}, u32[]{:S(2)}, u32[]{:S(2)}) %all-to-all-start) | async-done | bytes 1310752 | tf_op jit(solution)/shard_map/all_to_all | solution.py:152
  373.7 5.8 %collective-permute-start.23 = (f32[5,4,48,128]{3,2,1,0:T(8,128)S(1)}, f32[5,4,48,128]{3,2,1,0:T(8,128)S(1)}, u32[]{:S(2)}, u32[]{:S(2)}) collective-permute-start(f32[5,4,48,128]{3,2,1,0:T(8,128)S(1)} %pad_dynamic-slice_fusion.13), channel_id=1, source_target_pairs={{0,8},{3,9},{6,10},{9,11},{12,12},{15,13},{16,24},{19,25},{22,26},... | collective-permute-start | bytes 1474568 | tf_op jit(solution)/shard_map/ppermute | solution.py:164
  382.9 34.5 %collective-permute-done.21 = f32[5,4,48,128]{3,2,1,0:T(8,128)S(1)} collective-permute-done((f32[5,4,48,128]{3,2,1,0:T(8,128)S(1)}, f32[5,4,48,128]{3,2,1,0:T(8,128)S(1)}, u32[]{:S(2)}, u32[]{:S(2)}) %collective-permute-start.21) | collective-permute-done | bytes 491552 | tf_op jit(solution)/shard_map/ppermute | solution.py:164
  417.5 11.6 %collective-permute-done.25 = f32[5,4,48,128]{3,2,1,0:T(8,128)S(1)} collective-permute-done((f32[5,4,48,128]{3,2,1,0:T(8,128)S(1)}, f32[5,4,48,128]{3,2,1,0:T(8,128)S(1)}, u32[]{:S(2)}, u32[]{:S(2)}) %collective-permute-start.25) | collective-permute-done | bytes 491552 | tf_op jit(solution)/shard_map/ppermute | solution.py:164
  429.2 1.6 dynamic-slice_select_fusion
  (114 shorter events, 30.4 us)
Async XLA Ops:
  7.2 7.7 %copy-start = (f32[5,4,48,384]{3,2,1,0:T(8,128)S(1)}, f32[5,4,48,384]{3,2,1,0:T(8,128)}, u32[]{:S(2)}) copy-start(f32[5,4,48,384]{3,2,1,0:T(8,128)} %param.7) | copy-start | bytes 4423684
  7.2 199.3 %all-reduce.6.cloned.1.call-start = ((), (), s32[]{:S(2)}) async-start(), calls=%async_computation.1 | async-start | bytes 5898240
  9.6 35.7 %collective-permute-start.6 = (f32[5,4,48,1]{3,2,1,0:T(8,128)}, f32[5,4,48,1]{3,2,1,0:T(8,128)}, u32[]{:S(2)}, u32[]{:S(2)}) collective-permute-start(f32[5,4,48,1]{3,2,1,0:T(8,128)} %get-tuple-element.43), channel_id=1, source_target_pairs={{0,1},{1,2},{2,3},{3,4},{4,5},{5,6},{6,7},{7,8},{8,9},{9,10},{10,1... | collective-permute-start | bytes 11528 | tf_op jit(solution)/shard_map/ppermute | solution.py:22
  12.8 32.6 %collective-permute-start.7 = (f32[5,4,48,1]{3,2,1,0:T(8,128)}, f32[5,4,48,1]{3,2,1,0:T(8,128)}, u32[]{:S(2)}, u32[]{:S(2)}) collective-permute-start(f32[5,4,48,1]{3,2,1,0:T(8,128)} %get-tuple-element.44), channel_id=1, source_target_pairs={{1,0},{2,1},{3,2},{4,3},{5,4},{6,5},{7,6},{8,7},{9,8},{10,9},{11,1... | collective-permute-start | bytes 11528 | tf_op jit(solution)/shard_map/ppermute | solution.py:23
  15.6 28.2 %collective-permute-start.4 = (f32[5,4,1,384]{3,1,2,0:T(4,128)}, f32[5,4,1,384]{3,1,2,0:T(4,128)}, u32[]{:S(2)}, u32[]{:S(2)}) collective-permute-start(f32[5,4,1,384]{3,1,2,0:T(4,128)} %copy.324), channel_id=1, source_target_pairs={{0,16},{16,32},{32,48},{48,64},{64,80},{80,96},{96,112},{1,17},{17... | collective-permute-start | bytes 92168 | tf_op jit(solution)/shard_map/ppermute | solution.py:20
  20.4 24.1 %collective-permute-start.5 = (f32[5,4,1,384]{3,1,2,0:T(4,128)}, f32[5,4,1,384]{3,1,2,0:T(4,128)}, u32[]{:S(2)}, u32[]{:S(2)}) collective-permute-start(f32[5,4,1,384]{3,1,2,0:T(4,128)} %copy.325), channel_id=1, source_target_pairs={{16,0},{32,16},{48,32},{64,48},{80,64},{96,80},{112,96},{17,1},{33... | collective-permute-start | bytes 92168 | tf_op jit(solution)/shard_map/ppermute | solution.py:21
  24.1 2.1 copy-start.1
  26.2 1.8 copy-start.8
  26.2 2.7 copy-start.12
  49.4 1.4 copy-start.2
  49.4 9.6 %copy-start.9 = (f32[2,4,48,384]{3,2,1,0:T(8,128)S(1)}, f32[2,4,48,384]{3,2,1,0:T(8,128)}, u32[]{:S(2)}) copy-start(f32[2,4,48,384]{3,2,1,0:T(8,128)} %param.11) | copy-start | bytes 1769476
  50.8 22.4 %collective-permute-start.10 = (f32[5,4,48,130]{3,2,1,0:T(8,128)S(1)}, f32[5,4,48,130]{3,2,1,0:T(8,128)S(1)}, u32[]{:S(2)}, u32[]{:S(2)}) collective-permute-start(f32[5,4,48,130]{3,2,1,0:T(8,128)S(1)} %get-tuple-element.35), channel_id=1, source_target_pairs={{9,1},{10,4},{11,7},{12,10},{13,13},{25,17},{26,20},{27,23},{28,26... | collective-permute-start | bytes 1497608 | tf_op jit(solution)/shard_map/ppermute | solution.py:130
  53.0 29.0 %collective-permute-start.11 = (f32[5,4,48,130]{3,2,1,0:T(8,128)S(1)}, f32[5,4,48,130]{3,2,1,0:T(8,128)S(1)}, u32[]{:S(2)}, u32[]{:S(2)}) collective-permute-start(f32[5,4,48,130]{3,2,1,0:T(8,128)S(1)} %get-tuple-element.36), channel_id=1, source_target_pairs={{8,2},{9,5},{10,8},{11,11},{12,14},{24,18},{25,21},{26,24},{27,27}... | collective-permute-start | bytes 1497608 | tf_op jit(solution)/shard_map/ppermute | solution.py:130
  54.3 48.2 %collective-permute-start.12 = (f32[5,4,48,130]{3,2,1,0:T(8,128)S(1)}, f32[5,4,48,130]{3,2,1,0:T(8,128)S(1)}, u32[]{:S(2)}, u32[]{:S(2)}) collective-permute-start(f32[5,4,48,130]{3,2,1,0:T(8,128)S(1)} %get-tuple-element.37), channel_id=1, source_target_pairs={{9,2},{10,5},{11,8},{12,11},{13,14},{25,18},{26,21},{27,24},{28,27... | collective-permute-start | bytes 1497608 | tf_op jit(solution)/shard_map/ppermute | solution.py:130
  55.7 52.0 %collective-permute-start.8 = (f32[5,4,48,130]{3,2,1,0:T(8,128)S(1)}, f32[5,4,48,130]{3,2,1,0:T(8,128)S(1)}, u32[]{:S(2)}, u32[]{:S(2)}) collective-permute-start(f32[5,4,48,130]{3,2,1,0:T(8,128)S(1)} %get-tuple-element.38), channel_id=1, source_target_pairs={{8,0},{9,3},{10,6},{11,9},{12,12},{13,15},{24,16},{25,19},{26,22},... | collective-permute-start | bytes 1497608 | tf_op jit(solution)/shard_map/ppermute | solution.py:130
  57.6 52.2 %collective-permute-start.9 = (f32[5,4,48,130]{3,2,1,0:T(8,128)S(1)}, f32[5,4,48,130]{3,2,1,0:T(8,128)S(1)}, u32[]{:S(2)}, u32[]{:S(2)}) collective-permute-start(f32[5,4,48,130]{3,2,1,0:T(8,128)S(1)} %get-tuple-element.34), channel_id=1, source_target_pairs={{8,1},{9,4},{10,7},{11,10},{12,13},{24,17},{25,20},{26,23},{27,26}... | collective-permute-start | bytes 1497608 | tf_op jit(solution)/shard_map/ppermute | solution.py:130
  59.9 42.7 %copy-start.11 = (f32[5,4,1,384]{3,1,2,0:T(4,128)S(1)}, f32[5,4,1,384]{3,1,2,0:T(4,128)}, u32[]{:S(2)}) copy-start(f32[5,4,1,384]{3,1,2,0:T(4,128)} %copy.322) | copy-start | bytes 92164
  59.9 47.8 %copy-start.10 = (f32[5,4,1,384]{3,1,2,0:T(4,128)S(1)}, f32[5,4,1,384]{3,1,2,0:T(4,128)}, u32[]{:S(2)}) copy-start(f32[5,4,1,384]{3,1,2,0:T(4,128)} %copy.323) | copy-start | bytes 92164
  73.2 143.5 %collective-permute-start.2 = (f32[5,4,48,1]{3,2,1,0:T(8,128)}, f32[5,4,48,1]{3,2,1,0:T(8,128)}, u32[]{:S(2)}, u32[]{:S(2)}) collective-permute-start(f32[5,4,48,1]{3,2,1,0:T(8,128)} %get-tuple-element.30), channel_id=1, source_target_pairs={{0,1},{1,2},{2,3},{3,4},{4,5},{5,6},{6,7},{7,8},{8,9},{9,10},{10,1... | collective-permute-start | bytes 11528 | tf_op jit(solution)/shard_map/ppermute | solution.py:22
  81.9 134.7 %collective-permute-start.3 = (f32[5,4,48,1]{3,2,1,0:T(8,128)}, f32[5,4,48,1]{3,2,1,0:T(8,128)}, u32[]{:S(2)}, u32[]{:S(2)}) collective-permute-start(f32[5,4,48,1]{3,2,1,0:T(8,128)} %get-tuple-element.31), channel_id=1, source_target_pairs={{1,0},{2,1},{3,2},{4,3},{5,4},{6,5},{7,6},{8,7},{9,8},{10,9},{11,1... | collective-permute-start | bytes 11528 | tf_op jit(solution)/shard_map/ppermute | solution.py:23
  102.6 19.1 %collective-permute-start = (f32[5,4,1,384]{3,1,2,0:T(4,128)S(1)}, f32[5,4,1,384]{3,1,2,0:T(4,128)S(1)}, u32[]{:S(2)}, u32[]{:S(2)}) collective-permute-start(f32[5,4,1,384]{3,1,2,0:T(4,128)S(1)} %copy-done.11), channel_id=1, source_target_pairs={{0,16},{16,32},{32,48},{48,64},{64,80},{80,96},{96,112},{1,17},{17... | collective-permute-start | bytes 92168 | tf_op jit(solution)/shard_map/ppermute | solution.py:20
  107.7 14.7 %collective-permute-start.1 = (f32[5,4,1,384]{3,1,2,0:T(4,128)S(1)}, f32[5,4,1,384]{3,1,2,0:T(4,128)S(1)}, u32[]{:S(2)}, u32[]{:S(2)}) collective-permute-start(f32[5,4,1,384]{3,1,2,0:T(4,128)S(1)} %copy-done.10), channel_id=1, source_target_pairs={{16,0},{32,16},{48,32},{64,48},{80,64},{96,80},{112,96},{17,1},{33... | collective-permute-start | bytes 92168 | tf_op jit(solution)/shard_map/ppermute | solution.py:21
  118.3 2.8 copy-start.13
  221.3 14.6 %collective-permute-start.15 = (f32[5,4,48,1]{3,2,1,0:T(8,128)S(1)}, f32[5,4,48,1]{3,2,1,0:T(8,128)S(1)}, u32[]{:S(2)}, u32[]{:S(2)}) collective-permute-start(f32[5,4,48,1]{3,2,1,0:T(8,128)S(1)} %get-tuple-element.22), channel_id=1, source_target_pairs={{0,1},{1,2},{2,3},{3,4},{4,5},{5,6},{6,7},{7,8},{8,9},{9,10},{10,1... | collective-permute-start | bytes 11528 | tf_op jit(solution)/shard_map/ppermute | solution.py:22
  224.5 11.8 %collective-permute-start.16 = (f32[5,4,48,1]{3,2,1,0:T(8,128)S(1)}, f32[5,4,48,1]{3,2,1,0:T(8,128)S(1)}, u32[]{:S(2)}, u32[]{:S(2)}) collective-permute-start(f32[5,4,48,1]{3,2,1,0:T(8,128)S(1)} %get-tuple-element.23), channel_id=1, source_target_pairs={{1,0},{2,1},{3,2},{4,3},{5,4},{6,5},{7,6},{8,7},{9,8},{10,9},{11,1... | collective-permute-start | bytes 11528 | tf_op jit(solution)/shard_map/ppermute | solution.py:23
  226.7 7.0 %collective-permute-start.13 = (f32[5,4,1,384]{3,1,2,0:T(4,128)S(1)}, f32[5,4,1,384]{3,1,2,0:T(4,128)S(1)}, u32[]{:S(2)}, u32[]{:S(2)}) collective-permute-start(f32[5,4,1,384]{3,1,2,0:T(4,128)S(1)} %copy.310), channel_id=1, source_target_pairs={{0,16},{16,32},{32,48},{48,64},{64,80},{80,96},{96,112},{1,17},{17... | collective-permute-start | bytes 92168 | tf_op jit(solution)/shard_map/ppermute | solution.py:20
  230.3 6.0 %copy-start.4 = (f32[4,48,384]{2,1,0:T(8,128)S(1)}, f32[4,48,384]{2,1,0:T(8,128)}, u32[]{:S(2)}) copy-start(f32[4,48,384]{2,1,0:T(8,128)} %get-tuple-element.60) | copy-start | bytes 884740
  230.3 6.0 %copy-start.5 = (f32[4,48,384]{2,1,0:T(8,128)S(1)}, f32[4,48,384]{2,1,0:T(8,128)}, u32[]{:S(2)}) copy-start(f32[4,48,384]{2,1,0:T(8,128)} %get-tuple-element.61) | copy-start | bytes 884740
  230.3 6.0 %copy-start.6 = (f32[4,48,384]{2,1,0:T(8,128)S(1)}, f32[4,48,384]{2,1,0:T(8,128)}, u32[]{:S(2)}) copy-start(f32[4,48,384]{2,1,0:T(8,128)} %param.12) | copy-start | bytes 884740
  230.3 6.0 %copy-start.7 = (f32[48,384]{1,0:T(8,128)S(1)}, f32[48,384]{1,0:T(8,128)}, u32[]{:S(2)}) copy-start(f32[48,384]{1,0:T(8,128)} %multiply_add_fusion.4) | copy-start | bytes 221188
  230.3 5.6 %collective-permute-start.14 = (f32[5,4,1,384]{3,1,2,0:T(4,128)S(1)}, f32[5,4,1,384]{3,1,2,0:T(4,128)S(1)}, u32[]{:S(2)}, u32[]{:S(2)}) collective-permute-start(f32[5,4,1,384]{3,1,2,0:T(4,128)S(1)} %copy.312), channel_id=1, source_target_pairs={{16,0},{32,16},{48,32},{64,48},{80,64},{96,80},{112,96},{17,1},{33... | collective-permute-start | bytes 92168 | tf_op jit(solution)/shard_map/ppermute | solution.py:21
  238.6 16.6 %collective-permute-start.19 = (f32[5,4,48,1]{3,2,1,0:T(8,128)S(1)}, f32[5,4,48,1]{3,2,1,0:T(8,128)S(1)}, u32[]{:S(2)}, u32[]{:S(2)}) collective-permute-start(f32[5,4,48,1]{3,2,1,0:T(8,128)S(1)} %get-tuple-element.14), channel_id=1, source_target_pairs={{0,1},{1,2},{2,3},{3,4},{4,5},{5,6},{6,7},{7,8},{8,9},{9,10},{10,1... | collective-permute-start | bytes 11528 | tf_op jit(solution)/shard_map/ppermute | solution.py:22
  241.5 13.7 %collective-permute-start.20 = (f32[5,4,48,1]{3,2,1,0:T(8,128)S(1)}, f32[5,4,48,1]{3,2,1,0:T(8,128)S(1)}, u32[]{:S(2)}, u32[]{:S(2)}) collective-permute-start(f32[5,4,48,1]{3,2,1,0:T(8,128)S(1)} %get-tuple-element.15), channel_id=1, source_target_pairs={{1,0},{2,1},{3,2},{4,3},{5,4},{6,5},{7,6},{8,7},{9,8},{10,9},{11,1... | collective-permute-start | bytes 11528 | tf_op jit(solution)/shard_map/ppermute | solution.py:23
  244.6 7.7 %collective-permute-start.17 = (f32[5,4,1,384]{3,1,2,0:T(4,128)S(1)}, f32[5,4,1,384]{3,1,2,0:T(4,128)S(1)}, u32[]{:S(2)}, u32[]{:S(2)}) collective-permute-start(f32[5,4,1,384]{3,1,2,0:T(4,128)S(1)} %copy.315), channel_id=1, source_target_pairs={{0,16},{16,32},{32,48},{48,64},{64,80},{80,96},{96,112},{1,17},{17... | collective-permute-start | bytes 92168 | tf_op jit(solution)/shard_map/ppermute | solution.py:20
  249.6 5.5 %collective-permute-start.18 = (f32[5,4,1,384]{3,1,2,0:T(4,128)S(1)}, f32[5,4,1,384]{3,1,2,0:T(4,128)S(1)}, u32[]{:S(2)}, u32[]{:S(2)}) collective-permute-start(f32[5,4,1,384]{3,1,2,0:T(4,128)S(1)} %copy.317), channel_id=1, source_target_pairs={{16,0},{32,16},{48,32},{64,48},{80,64},{96,80},{112,96},{17,1},{33... | collective-permute-start | bytes 92168 | tf_op jit(solution)/shard_map/ppermute | solution.py:21
  341.3 28.9 %all-to-all-start = ((f32[8,5,4,16,128]{4,3,2,1,0:T(8,128)}), f32[8,5,4,16,128]{4,3,2,1,0:T(8,128)S(1)}, u32[]{:S(2)}, u32[]{:S(2)}) async-start(f32[8,5,4,16,128]{4,3,2,1,0:T(8,128)} %stack.79), calls=%async_computation | async-start | bytes 2621440 | tf_op jit(solution)/shard_map/all_to_all | solution.py:152
  370.4 46.9 %collective-permute-start.21 = (f32[5,4,48,128]{3,2,1,0:T(8,128)S(1)}, f32[5,4,48,128]{3,2,1,0:T(8,128)S(1)}, u32[]{:S(2)}, u32[]{:S(2)}) collective-permute-start(f32[5,4,48,128]{3,2,1,0:T(8,128)S(1)} %pad_dynamic-slice_fusion.13), channel_id=1, source_target_pairs={{1,9},{4,10},{7,11},{10,12},{13,13},{17,25},{20,26},{23,27},{26,28... | collective-permute-start | bytes 1474568 | tf_op jit(solution)/shard_map/ppermute | solution.py:164
  371.7 45.6 %collective-permute-start.22 = (f32[5,4,48,128]{3,2,1,0:T(8,128)S(1)}, f32[5,4,48,128]{3,2,1,0:T(8,128)S(1)}, u32[]{:S(2)}, u32[]{:S(2)}) collective-permute-start(f32[5,4,48,128]{3,2,1,0:T(8,128)S(1)} %pad_dynamic-slice_fusion.13), channel_id=1, source_target_pairs={{2,9},{5,10},{8,11},{11,12},{14,13},{18,25},{21,26},{24,27},{27,28... | collective-permute-start | bytes 1474568 | tf_op jit(solution)/shard_map/ppermute | solution.py:164
  373.7 43.8 %collective-permute-start.23 = (f32[5,4,48,128]{3,2,1,0:T(8,128)S(1)}, f32[5,4,48,128]{3,2,1,0:T(8,128)S(1)}, u32[]{:S(2)}, u32[]{:S(2)}) collective-permute-start(f32[5,4,48,128]{3,2,1,0:T(8,128)S(1)} %pad_dynamic-slice_fusion.13), channel_id=1, source_target_pairs={{0,8},{3,9},{6,10},{9,11},{12,12},{15,13},{16,24},{19,25},{22,26},... | collective-permute-start | bytes 1474568 | tf_op jit(solution)/shard_map/ppermute | solution.py:164
  380.2 37.3 %collective-permute-start.24 = (f32[5,4,48,128]{3,2,1,0:T(8,128)S(1)}, f32[5,4,48,128]{3,2,1,0:T(8,128)S(1)}, u32[]{:S(2)}, u32[]{:S(2)}) collective-permute-start(f32[5,4,48,128]{3,2,1,0:T(8,128)S(1)} %pad_dynamic-slice_fusion.13), channel_id=1, source_target_pairs={{1,8},{4,9},{7,10},{10,11},{13,12},{17,24},{20,25},{23,26},{26,27}... | collective-permute-start | bytes 1474568 | tf_op jit(solution)/shard_map/ppermute | solution.py:164
  381.6 47.5 %collective-permute-start.25 = (f32[5,4,48,128]{3,2,1,0:T(8,128)S(1)}, f32[5,4,48,128]{3,2,1,0:T(8,128)S(1)}, u32[]{:S(2)}, u32[]{:S(2)}) collective-permute-start(f32[5,4,48,128]{3,2,1,0:T(8,128)S(1)} %pad_dynamic-slice_fusion.13), channel_id=1, source_target_pairs={{2,8},{5,9},{8,10},{11,11},{14,12},{18,24},{21,25},{24,26},{27,27}... | collective-permute-start | bytes 1474568 | tf_op jit(solution)/shard_map/ppermute | solution.py:164
  417.4 11.7 %copy-start.3 = (f32[5,4,48,384]{3,2,1,0:T(8,128)S(1)}, f32[5,4,48,384]{3,2,1,0:T(8,128)}, u32[]{:S(2)}) copy-start(f32[5,4,48,384]{3,2,1,0:T(8,128)} %copy-done.2) | copy-start | bytes 4423684
Sparse Core Ops, SparseCore 0:
  118.4 88.0 all-reduce.5
